TPU v7x, 32 devices: a whole 2x2x4 slice. The times are simulated.
32 devices in a mesh: dp: 8 (over z, x), mp: 4 (over y, core).
Axes of the slice: x: 2, y: 2, z: 4, core: 2. Of those that a mesh axis runs over, the one named last changes fastest.
Arguments:
- patches: bfloat16 [9216, 3072], P('dp'), may hold values from -6 to 6
- weight: bfloat16 [3072, 1536], P(None, 'mp'), may hold values from -0.109375 to 0.109375
- conv_bias: float32 [1536], P('mp'), may hold values from -3 to 3
- cotangent: bfloat16 [9216, 1536], P('dp', 'mp'), may hold values from -0.0390625 to 0.0390625
- row_scale: float32 [3072], replicated, may hold values from 0.25 to 4
- col_scale: float32 [1536], P('mp'), may hold values from 0.25 to 4
Outputs:
- output: bfloat16 [9216, 1536], P('dp', 'mp')
- left_factor: float32 [3072, 3072], P('dp', 'mp')
- right_factor: float32 [1536, 1536], P('dp', 'mp')
- norm_pair: float32 [2], replicated
All inputs are finite; a program needn't handle non-finite values.
Results may differ from a plain program's by a relative error of at most 0.001.
Values sent between devices are 32-bit elements; how exact they have to be, the bound alone decides.
A program may use at most 64 MiB of HBM per device.

v0:
```python
import jax
import jax.numpy as jnp
from jax import lax
from jax.sharding import PartitionSpec as P

COUT = 1536
K = 3072


def shards(patches, weight, conv_bias, cotangent, row_scale, col_scale):
    output = (jnp.dot(patches, weight, preferred_element_type=jnp.float32) + conv_bias).astype(
        jnp.bfloat16
    )
    inner_width = patches.shape[1]
    strip_rows = inner_width // lax.axis_size("dp")
    local_grad = lax.dot_general(
        patches, cotangent, (((0,), (0,)), ((), ())), preferred_element_type=jnp.float32
    )
    weighted = local_grad * row_scale[:, None] * col_scale[None, :]
    small_sum = jnp.sum(weighted * weighted)
    column = lax.psum(local_grad, "dp")
    rows_here = lax.dynamic_slice_in_dim(column, lax.axis_index("dp") * strip_rows, strip_rows, 0)
    left_part = lax.dot_general(
        rows_here,
        column,
        (((1,), (1,)), ((), ())),
        precision=lax.Precision.HIGHEST,
        preferred_element_type=jnp.float32,
    )
    left_factor = lax.psum_scatter(left_part / COUT, "mp", scatter_dimension=1, tiled=True)
    full_strip = lax.all_gather(rows_here, "mp", axis=1, tiled=True)
    right_factor = lax.psum_scatter(
        lax.dot_general(
            full_strip,
            rows_here,
            (((0,), (0,)), ((), ())),
            precision=lax.Precision.HIGHEST,
            preferred_element_type=jnp.float32,
        )
        / K,
        "dp",
        scatter_dimension=0,
        tiled=True,
    )
    row_part = lax.dynamic_slice_in_dim(row_scale, lax.axis_index("dp") * strip_rows, strip_rows, 0)
    scaled_rows = rows_here * row_part[:, None] * col_scale[None, :]
    large_sum = jnp.sum(scaled_rows * scaled_rows)
    small_total, large_total = lax.psum((small_sum, large_sum), ("dp", "mp"))
    norm_pair = jnp.stack([small_total, large_total]) / (K * COUT)
    return (output, left_factor, right_factor, norm_pair)


def solution(mesh):
    in_specs = (P("dp", None), P(None, "mp"), P("mp"), P("dp", "mp"), P(), P("mp"))
    out_specs = (P("dp", "mp"), P("dp", "mp"), P("dp", "mp"), P())
    return jax.shard_map(shards, mesh=mesh, in_specs=in_specs, out_specs=out_specs, check_vma=False)
```

profile of v0, /device:TPU:0, one launch (start us, length us, event | category | flops | bytes accessed | tf_op | source)
XLA Modules:
  0.0 348.9 jit_solution(10241874328816004457)
XLA Ops:
  7.2 0.0 copy-start
  7.2 0.0 all-reduce.3.cloned.1.call-start
  7.2 10.4 %multiply_reduce_fusion = (f32[]{:T(128)}, f32[3072,384]{1,0:T(8,128)}) fusion(f32[384]{0:T(512)} %param.11, f32[3072]{0:T(1024)} %param.10, bf16[1152,3072]{1,0:T(8,128)(2,1)} %param.6, bf16[1152,384]{1,0:T(8,128)(2,1)} %param.9), kind=kOutput, calls=%fused_computation | convolution fusion | flops 2722627584 | bytes 12695044 | tf_op jit(solution)/shard_map/dot_general | solution.py:16
  17.6 0.0 copy-start.2
  17.6 0.0 all-reduce.3.cloned.1.call-update
  17.7 0.0 all-gather.2.cloned.1.call-start
  17.7 0.8 dynamic_slice.7
  18.5 171.7 %all-reduce.3.cloned.1.call-done = f32[3072,384]{1,0:T(8,128)} async-done(((f32[3072,384]{1,0:T(8,128)}), f32[3072,384]{1,0:T(8,128)}) %all-reduce.3.cloned.1.call-update) | async-done | bytes 4718608 | tf_op jit(solution)/shard_map/psum | solution.py:21
  190.2 0.0 copy-done.2
  190.2 2.6 multiply_reduce_fusion.1
  192.7 0.0 copy-start.1
  192.7 0.0 all-gather.2.cloned.1.call-update
  192.8 0.0 reduce-scatter.5.cloned.1.call-start
  192.8 23.2 %all-gather.2.cloned.1.call-done = f32[384,1536]{1,0:T(8,128)} async-done(((f32[384,384]{1,0:T(8,128)}), f32[384,1536]{1,0:T(8,128)}) %all-gather.2.cloned.1.call-update) | async-done | bytes 2359312 | tf_op jit(solution)/shard_map/all_gather | solution.py:31
  216.0 7.2 %convolution_multiply_fusion.1 = f32[1536,384]{1,0:T(8,128)} fusion(f32[384,1536]{1,0:T(8,128)} %all-gather.2.cloned.1.call-done, f32[384,384]{1,0:T(8,128)} %get-tuple-element.7), kind=kOutput, calls=%fused_computation.2 | convolution fusion | flops 2718498816 | bytes 5308416 | tf_op jit(solution)/shard_map/dot_general | solution.py:33
  223.3 0.0 reduce-scatter.5.cloned.1.call-update
  223.3 0.2 reduce-scatter.3.cloned.1.call-start
  223.5 0.0 copy-done.1
  223.5 11.0 %convolution_multiply_fusion = f32[384,3072]{1,0:T(8,128)} fusion(f32[384,384]{1,0:T(8,128)S(1)} %copy-done.1, f32[3072,384]{1,0:T(8,128)} %all-reduce.3.cloned.1.call-done), kind=kOutput, calls=%fused_computation.1 | convolution fusion | flops 5436997632 | bytes 10027008 | tf_op jit(solution)/shard_map/dot_general | solution.py:23
  234.5 0.0 copy-start.3
  234.5 0.0 reduce-scatter.3.cloned.1.call-update
  234.5 0.0 copy-done
  234.5 0.6 copy-done.3
  235.2 7.1 %fusion = bf16[1152,384]{1,0:T(8,128)(2,1)} fusion(bf16[1152,3072]{1,0:T(8,128)(2,1)} %param.6, bf16[3072,384]{1,0:T(8,128)(2,1)S(1)} %copy-done, f32[384]{0:T(512)S(1)} %copy-done.3), kind=kOutput, calls=%fused_computation.4 | convolution fusion | flops 2718793728 | bytes 10323456 | tf_op jit(solution)/shard_map/dot_general | solution.py:11
  242.2 39.6 %all-reduce = (f32[1]{0:T(128)}, f32[1]{0:T(128)}) all-reduce(f32[1]{0:T(128)} %bitcast.1, f32[1]{0:T(128)} %bitcast), channel_id=1, replica_groups=mesh['dp'=8,'mp'=4] {'dp','mp'}, use_global_device_ids=true, to_apply=%region_6.0 | all-reduce | flops 2 | bytes 16 | tf_op jit(solution)/shard_map/psum | solution.py:48
  281.8 1.8 maximum_multiply_fusion
  283.6 9.1 %reduce-scatter.5.cloned.1.call-done = f32[192,384]{1,0:T(8,128)} async-done(((f32[1536,384]{1,0:T(8,128)}), f32[192,384]{1,0:T(8,128)}) %reduce-scatter.5.cloned.1.call-update) | async-done | bytes 294928 | tf_op jit(solution)/shard_map/reduce_scatter | solution.py:32
  292.7 49.7 %reduce-scatter.3.cloned.1.call-done = f32[384,768]{1,0:T(8,128)} async-done(((f32[384,3072]{1,0:T(8,128)}), f32[384,768]{1,0:T(8,128)}) %reduce-scatter.3.cloned.1.call-update) | async-done | bytes 1179664 | tf_op jit(solution)/shard_map/reduce_scatter | solution.py:30
Async XLA Ops:
  7.2 227.3 %copy-start = (bf16[3072,384]{1,0:T(8,128)(2,1)S(1)}, bf16[3072,384]{1,0:T(8,128)(2,1)}, u32[]{:S(2)}) copy-start(bf16[3072,384]{1,0:T(8,128)(2,1)} %param.7) | copy-start | bytes 7077892
  7.2 183.0 %all-reduce.3.cloned.1.call-start = ((), (), s32[]{:S(2)}) async-start(), calls=%async_computation.2 | async-start | bytes 9437184 | tf_op jit(solution)/shard_map/psum | solution.py:21
  17.6 172.5 %copy-start.2 = (f32[384]{0:T(512)S(1)}, f32[384]{0:T(512)}, u32[]{:S(2)}) copy-start(f32[384]{0:T(512)} %param.11) | copy-start | bytes 4612
  17.7 198.3 %all-gather.2.cloned.1.call-start = ((), (), s32[]{:S(2)}) async-start(), calls=%async_computation.4 | async-start | bytes 2949120 | tf_op jit(solution)/shard_map/all_gather | solution.py:31
  192.7 30.8 %copy-start.1 = (f32[384,384]{1,0:T(8,128)S(1)}, f32[384,384]{1,0:T(8,128)}, u32[]{:S(2)}) copy-start(f32[384,384]{1,0:T(8,128)} %get-tuple-element.7) | copy-start | bytes 1769476
  192.8 99.9 %reduce-scatter.5.cloned.1.call-start = ((), (), s32[]{:S(2)}) async-start(), calls=%async_computation.5 | async-start | bytes 2654208 | tf_op jit(solution)/shard_map/reduce_scatter | solution.py:32
  223.3 119.1 %reduce-scatter.3.cloned.1.call-start = ((), (), s32[]{:S(2)}) async-start(), calls=%async_computation.3 | async-start | bytes 5898240 | tf_op jit(solution)/shard_map/reduce_scatter | solution.py:30
  234.5 0.7 copy-start.3
Sparse Core Ops, SparseCore 0:
  17.8 172.3 all-reduce.2
  192.9 23.0 all-gather.1
  223.4 69.2 reduce-scatter.4
  295.7 46.6 reduce-scatter.2
where the time goes:
time: 349 us
  waiting for transfers between devices  254 us (73%)
  blocking collectives  39.6 us (11%)
  matrix products  35.7 us (10%)
  between operations  13.8 us (4%)
  other arithmetic  4.38 us (1%)
    psum x1, waiting for transfers between devices, shards(): column = lax.psum(local_grad, 'dp')  172 us
    reduce_scatter x1, waiting for transfers between devices, shards(): lax.psum_scatter(left_part / COUT, 'mp', scatter_dimension=1, tiled=True)  49.7 us
    psum x1, blocking collectives, shards(): small_total, large_total = lax.psum((small_sum, large_sum), ('dp', 'mp'))  39.6 us
    all_gather x1, waiting for transfers between devices, shards(): full_strip = lax.all_gather(rows_here, 'mp', axis=1, tiled=True)  23.2 us
    dot_general x1, matrix products, shards(): lax.dot_general(rows_here, column, (((1,), (1,)), ((), ())), precision=la...  11 us
    dot_general x1, matrix products, shards(): lax.dot_general(patches, cotangent, (((0,), (0,)), ((), ())), preferred_e...  10.4 us
    reduce_scatter x1, waiting for transfers between devices, shards(): lax.psum_scatter(lax.dot_general(full_strip, rows_here, (((0,), (0,)), ((...  9.1 us
    dot_general x1, matrix products, shards(): lax.dot_general(full_strip, rows_here, (((0,), (0,)), ((), ())), precisio...  7.25 us
  transfers between devices with their start and end apart: 4, of which 4 were waited for; matrix products, arithmetic and copies ran while one was open for 6% of the time, Pallas kernels for 0%

commit v1 on v0

--- a/solution.py
+++ b/solution.py
@@ -18,7 +18,7 @@
     )
     weighted = local_grad * row_scale[:, None] * col_scale[None, :]
     small_sum = jnp.sum(weighted * weighted)
-    column = lax.psum(local_grad, "dp")
+    column = jnp.sum(lax.all_gather(local_grad, "dp"), axis=0)
     rows_here = lax.dynamic_slice_in_dim(column, lax.axis_index("dp") * strip_rows, strip_rows, 0)
     left_part = lax.dot_general(
         rows_here,

time: 349 us -> 913 us (2.62)
  waiting for transfers between devices: 254 us -> 801 us
  other arithmetic: 4.38 us -> 20.3 us
    all_gather x0 -> x1, waiting for transfers between devices: none -> 718 us  [shards(): column = jnp.sum(lax.all_gather(local_grad, 'dp'), axis=0)]
    psum x1 -> x0, waiting for transfers between devices: 172 us -> none  [shards(): column = lax.psum(local_grad, 'dp')]
    reduce_sum x0 -> x1, other arithmetic: none -> 15.8 us  [shards(): column = jnp.sum(lax.all_gather(local_grad, 'dp'), axis=0)]
  transfers between devices with their start and end apart: 4 -> 4, of which waited for: 4 -> 4; matrix products, arithmetic and copies ran while one was open for 6% -> 2% of each run, Pallas kernels for 0% -> 0%
where the time goes in v1:
time: 913 us; the launch traced here: 912 us
  waiting for transfers between devices  801 us (88%)
  blocking collectives  39.7 us (4%)
  matrix products  35.7 us (4%)
  other arithmetic  20.3 us (2%)
  between operations  13.8 us (2%)
    all_gather x1, waiting for transfers between devices, shards(): column = jnp.sum(lax.all_gather(local_grad, 'dp'), axis=0)  718 us
    reduce_scatter x1, waiting for transfers between devices, shards(): lax.psum_scatter(left_part / COUT, 'mp', scatter_dimension=1, tiled=True)  49.7 us
    psum x1, blocking collectives, shards(): small_total, large_total = lax.psum((small_sum, large_sum), ('dp', 'mp'))  39.7 us
    all_gather x1, waiting for transfers between devices, shards(): full_strip = lax.all_gather(rows_here, 'mp', axis=1, tiled=True)  24.2 us
  transfers between devices with their start and end apart: 4, of which 4 were waited for; matrix products, arithmetic and copies ran while one was open for 2% of the time, Pallas kernels for 0%

profile of v1, /device:TPU:0, one launch (start us, length us, event | category | flops | bytes accessed | tf_op | source)
XLA Modules:
  0.0 912.4 jit_solution(8548829471799162508)
XLA Ops:
  7.2 0.0 copy-start
  7.2 0.0 all-gather.6.cloned.1.call-start
  7.2 10.5 %multiply_reduce_fusion = (f32[]{:T(128)}, f32[3072,384]{1,0:T(8,128)}) fusion(f32[384]{0:T(512)} %param.11, f32[3072]{0:T(1024)} %param.10, bf16[1152,3072]{1,0:T(8,128)(2,1)} %param.6, bf16[1152,384]{1,0:T(8,128)(2,1)} %param.9), kind=kOutput, calls=%fused_computation | convolution fusion | flops 2722627584 | bytes 12695044 | tf_op jit(solution)/shard_map/dot_general | solution.py:16
  17.7 0.0 all-gather.6.cloned.1.call-update
  17.7 0.0 all-gather.4.cloned.1.call-start
  17.8 0.8 dynamic_slice.7
  18.5 718.4 %all-gather.6.cloned.1.call-done = f32[24576,384]{1,0:T(8,128)} async-done(((f32[3072,384]{1,0:T(8,128)}), f32[24576,384]{1,0:T(8,128)}) %all-gather.6.cloned.1.call-update) | async-done | bytes 37748752 | tf_op jit(solution)/shard_map/all_gather | solution.py:21
  736.9 0.0 copy-start.2
  736.9 15.8 %reduce_sum.27 = f32[3072,384]{1,0:T(8,128)} reduce(f32[8,3072,384]{2,1,0:T(8,128)} %bitcast.11, f32[]{:T(128)} %constant.5.clone.1), dimensions={0}, to_apply=%region_0.0 | reduce | flops 8257536 | bytes 42467332 | tf_op jit(solution)/shard_map/reduce_sum | solution.py:21
  752.8 0.0 copy-done.2
  752.8 2.5 multiply_reduce_fusion.1
  755.3 0.0 copy-start.1
  755.3 0.0 all-gather.4.cloned.1.call-update
  755.3 0.0 reduce-scatter.5.cloned.1.call-start
  755.4 24.2 %all-gather.4.cloned.1.call-done = f32[384,1536]{1,0:T(8,128)} async-done(((f32[384,384]{1,0:T(8,128)}), f32[384,1536]{1,0:T(8,128)}) %all-gather.4.cloned.1.call-update) | async-done | bytes 2359312 | tf_op jit(solution)/shard_map/all_gather | solution.py:31
  779.5 7.2 convolution_multiply_fusion.1
  786.8 0.0 reduce-scatter.5.cloned.1.call-update
  786.8 0.2 reduce-scatter.3.cloned.1.call-start
  787.0 0.0 copy-done.1
  787.0 11.0 %convolution_multiply_fusion = f32[384,3072]{1,0:T(8,128)} fusion(f32[384,384]{1,0:T(8,128)S(1)} %copy-done.1, f32[3072,384]{1,0:T(8,128)} %reduce_sum.27), kind=kOutput, calls=%fused_computation.1 | convolution fusion | flops 5436997632 | bytes 10027008 | tf_op jit(solution)/shard_map/dot_general | solution.py:23
  798.0 0.0 copy-start.3
  798.0 0.0 reduce-scatter.3.cloned.1.call-update
  798.0 0.0 copy-done
  798.0 0.6 copy-done.3
  798.7 7.1 fusion
  805.7 39.7 %all-reduce = (f32[1]{0:T(128)}, f32[1]{0:T(128)}) all-reduce(f32[1]{0:T(128)} %bitcast.2, f32[1]{0:T(128)} %bitcast.1), channel_id=1, replica_groups=mesh['dp'=8,'mp'=4] {'dp','mp'}, use_global_device_ids=true, to_apply=%region_6.0 | all-reduce | flops 2 | bytes 16 | tf_op jit(solution)/shard_map/psum | solution.py:48
  845.4 2.0 maximum_multiply_fusion
  847.4 8.8 reduce-scatter.5.cloned.1.call-done
  856.2 49.7 %reduce-scatter.3.cloned.1.call-done = f32[384,768]{1,0:T(8,128)} async-done(((f32[384,3072]{1,0:T(8,128)}), f32[384,768]{1,0:T(8,128)}) %reduce-scatter.3.cloned.1.call-update) | async-done | bytes 1179664 | tf_op jit(solution)/shard_map/reduce_scatter | solution.py:30
Async XLA Ops:
  7.2 790.8 %copy-start = (bf16[3072,384]{1,0:T(8,128)(2,1)S(1)}, bf16[3072,384]{1,0:T(8,128)(2,1)}, u32[]{:S(2)}) copy-start(bf16[3072,384]{1,0:T(8,128)(2,1)} %param.7) | copy-start | bytes 7077892
  7.2 729.8 %all-gather.6.cloned.1.call-start = ((), (), s32[]{:S(2)}) async-start(), calls=%async_computation.5 | async-start | bytes 42467328 | tf_op jit(solution)/shard_map/all_gather | solution.py:21
  17.7 761.8 %all-gather.4.cloned.1.call-start = ((), (), s32[]{:S(2)}) async-start(), calls=%async_computation.3 | async-start | bytes 2949120 | tf_op jit(solution)/shard_map/all_gather | solution.py:31
  736.9 15.8 %copy-start.2 = (f32[384]{0:T(512)S(1)}, f32[384]{0:T(512)}, u32[]{:S(2)}) copy-start(f32[384]{0:T(512)} %param.11) | copy-start | bytes 4612
  755.3 31.7 %copy-start.1 = (f32[384,384]{1,0:T(8,128)S(1)}, f32[384,384]{1,0:T(8,128)}, u32[]{:S(2)}) copy-start(f32[384,384]{1,0:T(8,128)} %get-tuple-element.7) | copy-start | bytes 1769476
  755.3 100.9 %reduce-scatter.5.cloned.1.call-start = ((), (), s32[]{:S(2)}) async-start(), calls=%async_computation.4 | async-start | bytes 2654208 | tf_op jit(solution)/shard_map/reduce_scatter | solution.py:32
  786.8 119.1 %reduce-scatter.3.cloned.1.call-start = ((), (), s32[]{:S(2)}) async-start(), calls=%async_computation.2 | async-start | bytes 5898240 | tf_op jit(solution)/shard_map/reduce_scatter | solution.py:30
  798.0 0.7 copy-start.3
Sparse Core Ops, SparseCore 0:
  17.8 719.0 all-gather.5
  755.5 24.0 all-gather.3
  786.9 69.2 reduce-scatter.4
  859.2 46.6 reduce-scatter.2

commit v2 on v0

--- a/solution.py
+++ b/solution.py
@@ -28,7 +28,12 @@
         preferred_element_type=jnp.float32,
     )
     left_factor = lax.psum_scatter(left_part / COUT, "mp", scatter_dimension=1, tiled=True)
-    full_strip = lax.all_gather(rows_here, "mp", axis=1, tiled=True)
+    ring = [rows_here]
+    for hop in range(3):
+        ring.append(lax.ppermute(ring[-1], "mp", [(dev, (dev + 1) % 4) for dev in range(4)]))
+    full_strip = jnp.roll(
+        jnp.concatenate(ring[::-1], axis=1), (lax.axis_index("mp") + 1) * ring[0].shape[1], axis=1
+    )
     right_factor = lax.psum_scatter(
         lax.dot_general(
             full_strip,

time: 349 us -> 357 us (1.023)
  local copies, waits for them, and re-layouts: 1.44 us -> 6.25 us
  waiting for transfers between devices: 254 us -> 258 us
    ppermute x0 -> x3, waiting for transfers between devices: none -> 28.3 us  [shards(): lax.ppermute(ring[-1], 'mp', [(dev, (dev + 1) % 4) for dev in range(4)])]
    all_gather x1 -> x0, waiting for transfers between devices: 23.2 us -> none  [shards(): full_strip = lax.all_gather(rows_here, 'mp', axis=1, tiled=True)]
    unnamed x8 -> x13, local copies, waits for them, and re-layouts: 0.66 us -> 5.4 us
  transfers between devices with their start and end apart: 4 -> 6, of which waited for: 4 -> 6; matrix products, arithmetic and copies ran while one was open for 6% -> 6% of each run, Pallas kernels for 0% -> 0%
where the time goes in v2:
time: 357 us
  waiting for transfers between devices  258 us (72%)
  blocking collectives  39.5 us (11%)
  matrix products  35.2 us (10%)
  between operations  13.8 us (4%)
  local copies, waits for them, and re-layouts  6.25 us (2%)
  other arithmetic  3.69 us (1%)
    psum x1, waiting for transfers between devices, shards(): column = lax.psum(local_grad, 'dp')  172 us
    reduce_scatter x1, waiting for transfers between devices, shards(): lax.psum_scatter(left_part / COUT, 'mp', scatter_dimension=1, tiled=True)  49.7 us
    psum x1, blocking collectives, shards(): small_total, large_total = lax.psum((small_sum, large_sum), ('dp', 'mp'))  39.5 us
    ppermute x3, waiting for transfers between devices, shards(): lax.ppermute(ring[-1], 'mp', [(dev, (dev + 1) % 4) for dev in range(4)])  28.3 us
    dot_general x1, matrix products, shards(): lax.dot_general(rows_here, column, (((1,), (1,)), ((), ())), precision=la...  11 us
    dot_general x1, matrix products, shards(): lax.dot_general(patches, cotangent, (((0,), (0,)), ((), ())), preferred_e...  10.5 us
    reduce_scatter x1, waiting for transfers between devices, shards(): lax.psum_scatter(lax.dot_general(full_strip, rows_here, (((0,), (0,)), ((...  8.32 us
  transfers between devices with their start and end apart: 6, of which 6 were waited for; matrix products, arithmetic and copies ran while one was open for 6% of the time, Pallas kernels for 0%

profile of v2, /device:TPU:0, one launch (start us, length us, event | category | flops | bytes accessed | tf_op | source)
XLA Modules:
  0.0 356.8 jit_solution(11939947567226541536)
XLA Ops:
  7.2 0.0 copy-start
  7.2 0.0 all-reduce.3.cloned.1.call-start
  7.2 10.5 %multiply_reduce_fusion = (f32[]{:T(128)}, f32[3072,384]{1,0:T(8,128)}) fusion(f32[384]{0:T(512)} %param.11, f32[3072]{0:T(1024)} %param.10, bf16[1152,3072]{1,0:T(8,128)(2,1)} %param.6, bf16[1152,384]{1,0:T(8,128)(2,1)} %param.9), kind=kOutput, calls=%fused_computation | convolution fusion | flops 2722627584 | bytes 12695044 | tf_op jit(solution)/shard_map/dot_general | solution.py:16
  17.7 0.0 copy-start.1
  17.7 0.0 all-reduce.3.cloned.1.call-update
  17.7 0.0 reduce-scatter.5.cloned.1.call-start
  17.8 0.8 dynamic_slice.12
  18.6 171.7 %all-reduce.3.cloned.1.call-done = f32[3072,384]{1,0:T(8,128)} async-done(((f32[3072,384]{1,0:T(8,128)}), f32[3072,384]{1,0:T(8,128)}) %all-reduce.3.cloned.1.call-update) | async-done | bytes 4718608 | tf_op jit(solution)/shard_map/psum | solution.py:21
  190.2 0.0 copy-done.1
  190.2 1.9 multiply_reduce_fusion.1
  192.1 0.0 collective-permute-start
  192.2 9.3 %collective-permute-done = f32[384,384]{1,0:T(8,128)S(1)} collective-permute-done((f32[384,384]{1,0:T(8,128)S(1)}, f32[384,384]{1,0:T(8,128)S(1)}, u32[]{:S(2)}, u32[]{:S(2)}) %collective-permute-start) | collective-permute-done | bytes 589856 | tf_op jit(solution)/shard_map/ppermute | solution.py:33
  201.5 0.0 collective-permute-start.1
  201.5 9.4 %collective-permute-done.1 = f32[384,384]{1,0:T(8,128)} collective-permute-done((f32[384,384]{1,0:T(8,128)S(1)}, f32[384,384]{1,0:T(8,128)}, u32[]{:S(2)}, u32[]{:S(2)}) %collective-permute-start.1) | collective-permute-done | bytes 589856 | tf_op jit(solution)/shard_map/ppermute | solution.py:33
  210.9 0.0 collective-permute-start.2
  210.9 9.6 %collective-permute-done.2 = f32[384,384]{1,0:T(8,128)} collective-permute-done((f32[384,384]{1,0:T(8,128)}, f32[384,384]{1,0:T(8,128)}, u32[]{:S(2)}, u32[]{:S(2)}) %collective-permute-start.2) | collective-permute-done | bytes 589856 | tf_op jit(solution)/shard_map/ppermute | solution.py:33
  220.5 1.1 constant_dynamic-update-slice_fusion.7
  221.6 1.1 constant_dynamic-update-slice_fusion.6
  222.8 0.1 constant_dynamic-update-slice_fusion.5
  222.8 0.1 constant_dynamic-update-slice_fusion.4
  222.9 1.1 constant_dynamic-update-slice_fusion.3
  224.1 1.1 constant_dynamic-update-slice_fusion.2
  225.2 0.1 constant_dynamic-update-slice_fusion.1
  225.3 0.1 constant_dynamic-update-slice_fusion
  225.4 6.7 %convolution_multiply_fusion.1 = f32[1536,384]{1,0:T(8,128)} fusion(f32[384,384]{1,0:T(8,128)S(1)} %get-tuple-element.7, f32[384,3072]{1,0:T(8,128)S(1)} %constant_dynamic-update-slice_fusion, s32[]{:T(128)S(6)} %select_n.19), kind=kOutput, calls=%fused_computation.2 | convolution fusion | flops 2718498816 | bytes 5308420 | tf_op jit(solution)/shard_map/dot_general | solution.py:38
  232.1 0.0 reduce-scatter.5.cloned.1.call-update
  232.1 0.2 reduce-scatter.3.cloned.1.call-start
  232.3 11.0 %convolution_multiply_fusion = f32[384,3072]{1,0:T(8,128)} fusion(f32[384,384]{1,0:T(8,128)S(1)} %get-tuple-element.7, f32[3072,384]{1,0:T(8,128)} %all-reduce.3.cloned.1.call-done), kind=kOutput, calls=%fused_computation.1 | convolution fusion | flops 5436997632 | bytes 10027008 | tf_op jit(solution)/shard_map/dot_general | solution.py:23
  243.3 0.0 copy-start.2
  243.3 0.0 reduce-scatter.3.cloned.1.call-update
  243.3 0.0 copy-done
  243.3 0.6 copy-done.2
  243.9 7.1 %fusion = bf16[1152,384]{1,0:T(8,128)(2,1)} fusion(bf16[1152,3072]{1,0:T(8,128)(2,1)} %param.6, bf16[3072,384]{1,0:T(8,128)(2,1)S(1)} %copy-done, f32[384]{0:T(512)S(1)} %copy-done.2), kind=kOutput, calls=%fused_computation.4 | convolution fusion | flops 2718793728 | bytes 10323456 | tf_op jit(solution)/shard_map/dot_general | solution.py:11
  251.0 39.5 %all-reduce = (f32[1]{0:T(128)}, f32[1]{0:T(128)}) all-reduce(f32[1]{0:T(128)} %bitcast.1, f32[1]{0:T(128)} %bitcast), channel_id=1, replica_groups=mesh['dp'=8,'mp'=4] {'dp','mp'}, use_global_device_ids=true, to_apply=%region_6.7 | all-reduce | flops 2 | bytes 16 | tf_op jit(solution)/shard_map/psum | solution.py:53
  290.5 1.8 maximum_multiply_fusion
  292.3 8.3 %reduce-scatter.5.cloned.1.call-done = f32[192,384]{1,0:T(8,128)} async-done(((f32[1536,384]{1,0:T(8,128)}), f32[192,384]{1,0:T(8,128)}) %reduce-scatter.5.cloned.1.call-update) | async-done | bytes 294928 | tf_op jit(solution)/shard_map/reduce_scatter | solution.py:37
  300.6 49.7 %reduce-scatter.3.cloned.1.call-done = f32[384,768]{1,0:T(8,128)} async-done(((f32[384,3072]{1,0:T(8,128)}), f32[384,768]{1,0:T(8,128)}) %reduce-scatter.3.cloned.1.call-update) | async-done | bytes 1179664 | tf_op jit(solution)/shard_map/reduce_scatter | solution.py:30
Async XLA Ops:
  7.2 236.1 %copy-start = (bf16[3072,384]{1,0:T(8,128)(2,1)S(1)}, bf16[3072,384]{1,0:T(8,128)(2,1)}, u32[]{:S(2)}) copy-start(bf16[3072,384]{1,0:T(8,128)(2,1)} %param.7) | copy-start | bytes 7077892
  7.2 183.1 %all-reduce.3.cloned.1.call-start = ((), (), s32[]{:S(2)}) async-start(), calls=%async_computation.2 | async-start | bytes 9437184 | tf_op jit(solution)/shard_map/psum | solution.py:21
  17.7 172.5 %copy-start.1 = (f32[384]{0:T(512)S(1)}, f32[384]{0:T(512)}, u32[]{:S(2)}) copy-start(f32[384]{0:T(512)} %param.11) | copy-start | bytes 4612
  17.7 282.9 %reduce-scatter.5.cloned.1.call-start = ((), (), s32[]{:S(2)}) async-start(), calls=%async_computation.4 | async-start | bytes 2654208 | tf_op jit(solution)/shard_map/reduce_scatter | solution.py:37
  192.1 9.3 %collective-permute-start = (f32[384,384]{1,0:T(8,128)S(1)}, f32[384,384]{1,0:T(8,128)S(1)}, u32[]{:S(2)}, u32[]{:S(2)}) collective-permute-start(f32[384,384]{1,0:T(8,128)S(1)} %get-tuple-element.7), channel_id=1, source_target_pairs={{0,1},{1,2},{2,3},{3,0},{4,5},{5,6},{6,7},{7,4},{8,9},{9,10},{10,1... | collective-permute-start | bytes 1769480 | tf_op jit(solution)/shard_map/ppermute | solution.py:33
  201.5 9.4 %collective-permute-start.1 = (f32[384,384]{1,0:T(8,128)S(1)}, f32[384,384]{1,0:T(8,128)}, u32[]{:S(2)}, u32[]{:S(2)}) collective-permute-start(f32[384,384]{1,0:T(8,128)S(1)} %collective-permute-done), channel_id=1, source_target_pairs={{0,1},{1,2},{2,3},{3,0},{4,5},{5,6},{6,7},{7,4},{8,9},{9,10},{10,1... | collective-permute-start | bytes 1769480 | tf_op jit(solution)/shard_map/ppermute | solution.py:33
  210.9 9.6 %collective-permute-start.2 = (f32[384,384]{1,0:T(8,128)}, f32[384,384]{1,0:T(8,128)}, u32[]{:S(2)}, u32[]{:S(2)}) collective-permute-start(f32[384,384]{1,0:T(8,128)} %collective-permute-done.1), channel_id=1, source_target_pairs={{0,1},{1,2},{2,3},{3,0},{4,5},{5,6},{6,7},{7,4},{8,9},{9,10},{10,1... | collective-permute-start | bytes 1769480 | tf_op jit(solution)/shard_map/ppermute | solution.py:33
  232.1 118.2 %reduce-scatter.3.cloned.1.call-start = ((), (), s32[]{:S(2)}) async-start(), calls=%async_computation.3 | async-start | bytes 5898240 | tf_op jit(solution)/shard_map/reduce_scatter | solution.py:30
  243.3 0.7 copy-start.2
Sparse Core Ops, SparseCore 0:
  17.8 172.3 all-reduce.2
  232.2 68.3 reduce-scatter.4
  303.7 46.4 reduce-scatter.2
